TPU v7x, 32 devices: a whole 2x2x4 slice. The times are simulated.
32 devices in a mesh: dp: 8 (over z, x), mp: 4 (over y, core).
Axes of the slice: x: 2, y: 2, z: 4, core: 2. Of those that a mesh axis runs over, the one named last changes fastest.
Arguments:
- activations: bfloat16 [4096, 3072], P('dp', 'mp'), may hold values from -6 to 6
- out_grads: bfloat16 [4096, 6144], P('dp', 'mp'), may hold values from -0.25 to 0.25
- error: bfloat16 [8, 3072, 6144], P('dp', 'mp'), may hold values from -8 to 8
- sketch: bfloat16 [6144, 64], replicated, may hold values from -0.078125 to 0.078125
- momentum: float32 [3072, 6144], P('mp', 'dp'), may hold values from -6 to 6
Outputs:
- error_new: bfloat16 [8, 3072, 6144], P('dp', 'mp')
- momentum_new: float32 [3072, 6144], P('mp', 'dp')
- next_sketch: bfloat16 [6144, 64], replicated
All inputs are finite; a program needn't handle non-finite values.
Results may differ from a plain program's by a relative error of at most 0.0057.
Values may be sent and summed in bfloat16 or wider, within the bound.
A program may use at most 64 MiB of HBM per device.

v0:
```python
import jax
import jax.numpy as jnp
from jax import lax
from jax.sharding import PartitionSpec as P

beta_decay = 0.9


def update_momentum(momentum, basis_rows, sketch_block):
    product = lax.dot_general(
        basis_rows, sketch_block, (((1,), (1,)), ((), ())), preferred_element_type=jnp.float32
    )
    return beta_decay * momentum + product


def local(activations, out_grads, error, sketch, momentum):
    own_error = error[0]
    product = lax.dot_general(
        activations,
        lax.all_gather(out_grads, "mp", axis=1, tiled=True),
        (((0,), (0,)), ((), ())),
        preferred_element_type=jnp.float32,
    )
    accumulated = (product + own_error.astype(jnp.float32)).astype(jnp.bfloat16)
    local_left = jnp.dot(accumulated, sketch, preferred_element_type=jnp.float32)
    left_sketch = lax.psum(local_left, "dp")
    gram_local = jnp.dot(
        left_sketch.T,
        left_sketch,
        precision=lax.Precision.HIGHEST,
        preferred_element_type=jnp.float32,
    )
    gram_matrix = lax.psum(gram_local, "mp")
    factor = jnp.linalg.cholesky(gram_matrix)
    basis_rows = jax.scipy.linalg.solve_triangular(factor, left_sketch.T, lower=True).T.astype(
        jnp.bfloat16
    )
    block_width = momentum.shape[1]
    local_right = lax.dot_general(
        accumulated, basis_rows, (((0,), (0,)), ((), ())), preferred_element_type=jnp.float32
    )
    right_sketch = lax.psum(local_right, ("dp", "mp"))
    next_sketch = right_sketch.astype(jnp.bfloat16)
    sketch_part = lax.dynamic_slice_in_dim(
        next_sketch, lax.axis_index("dp") * block_width, block_width, 0
    )
    momentum_new = update_momentum(momentum, basis_rows, sketch_part)
    decoded = lax.dot_general(
        basis_rows, next_sketch, (((1,), (1,)), ((), ())), preferred_element_type=jnp.float32
    )
    error_new = (accumulated.astype(jnp.float32) - decoded / lax.axis_size("dp")).astype(
        jnp.bfloat16
    )
    return (error_new[None], momentum_new, next_sketch)


def solution(mesh):
    in_specs = (P("dp", "mp"), P("dp", "mp"), P("dp", "mp", None), P(), P("mp", "dp"))
    out_specs = (P("dp", "mp", None), P("mp", "dp"), P())
    return jax.shard_map(local, mesh=mesh, in_specs=in_specs, out_specs=out_specs, check_vma=False)
```

profile of v0, /device:TPU:0, one launch (start us, length us, event | category | flops | bytes accessed | tf_op | source)
XLA Modules:
  0.0 249.4 jit_solution(14047941913646381180)
XLA Ops:
  7.2 0.0 copy-start
  7.2 0.0 all-gather.2.cloned.1.call-start
  7.2 0.7 all-gather.2.cloned.1.call-update
  7.9 0.0 copy-start.4
  7.9 0.0 all-reduce.3.cloned.1.call-start
  8.0 50.7 %all-gather.2.cloned.1.call-done = bf16[512,6144]{1,0:T(8,128)(2,1)} async-done(((bf16[512,1536]{1,0:T(8,128)(2,1)}), bf16[512,6144]{1,0:T(8,128)(2,1)}) %all-gather.2.cloned.1.call-update) | async-done | bytes 6291472 | tf_op jit(solution)/shard_map/all_gather | solution.py:20
  58.7 0.0 copy-done
  58.7 9.6 %fusion = bf16[768,6144]{1,0:T(8,128)(2,1)S(1)} fusion(bf16[1,768,6144]{2,1,0:T(8,128)(2,1)} %param.7, bf16[512,768]{1,0:T(8,128)(2,1)S(1)} %copy-done, bf16[512,6144]{1,0:T(8,128)(2,1)} %all-gather.2.cloned.1.call-done), kind=kOutput, calls=%fused_computation.1 | convolution fusion | flops 4845993984 | bytes 25952256 | tf_op jit(solution)/shard_map/dot_general | solution.py:18
  68.3 0.0 copy-start.1
  68.3 3.7 %copy-done.1 = bf16[768,6144]{1,0:T(8,128)(2,1)} copy-done((bf16[768,6144]{1,0:T(8,128)(2,1)}, bf16[768,6144]{1,0:T(8,128)(2,1)S(1)}, u32[]{:S(2)}) %copy-start.1) | copy-done | bytes 9437208
  72.1 0.0 copy-done.4
  72.1 3.7 %fusion.7 = f32[768,64]{0,1:T(8,128)} fusion(bf16[768,6144]{1,0:T(8,128)(2,1)S(1)} %fusion, bf16[6144,64]{0,1:T(8,128)(2,1)S(1)} %copy-done.4), kind=kOutput, calls=%fused_computation.17 | convolution fusion | flops 603979776 | bytes 10420224 | tf_op jit(solution)/shard_map/dot_general | solution.py:25
  75.7 0.0 all-reduce.3.cloned.1.call-update
  75.8 70.8 %all-reduce.3.cloned.1.call-done = f32[768,64]{0,1:T(8,128)} async-done(((f32[768,64]{0,1:T(8,128)}), f32[768,64]{0,1:T(8,128)}) %all-reduce.3.cloned.1.call-update) | async-done | bytes 196624 | tf_op jit(solution)/shard_map/psum | solution.py:26
  146.6 1.3 fusion.8
  147.9 10.3 %psum.22 = f32[64,64]{0,1:T(8,128)S(1)} all-reduce(f32[64,64]{0,1:T(8,128)S(1)} %fusion.8), channel_id=1, replica_groups=mesh['dp'=8,'mp'=4] {'mp'}, use_global_device_ids=true, to_apply=%region_1.0 | all-reduce | flops 4096 | bytes 32768 | tf_op jit(solution)/shard_map/psum | solution.py:33
  158.2 0.1 copy.9
  158.3 5.8 %cholesky.16 = f32[64,64]{1,0:T(8,128)S(1)} custom-call(f32[64,64]{1,0:T(8,128)S(1)} %fusion.5), custom_call_target="Cholesky" | custom-call | tf_op jit(solution)/shard_map/jit(cholesky)/cholesky | solution.py:34
  164.2 0.6 compare_reduce_fusion
  164.8 0.7 fusion.3
  165.5 4.9 %custom-call.7 = f32[1,64,64]{1,2,0:T(8,128)S(1)} custom-call(f32[1,64,64]{2,1,0:T(8,128)S(1)} %fusion.3), custom_call_target="InvertDiagBlocksLowerTriangular" | custom-call | tf_op jit(solution)/shard_map/jit(_solve_triangular)/triangular_solve | solution.py:35
  170.4 1.3 convolution_convert_fusion
  171.7 5.4 %fusion.9 = f32[6144,64]{0,1:T(8,128)S(1)} fusion(bf16[768,64]{0,1:T(8,128)(2,1)S(1)} %convolution_convert_fusion, bf16[768,6144]{1,0:T(8,128)(2,1)} %copy-done.1), kind=kOutput, calls=%fused_computation.19 | convolution fusion | flops 603979776 | bytes 11108352 | tf_op jit(solution)/shard_map/dot_general | solution.py:39
  177.1 55.7 %all-reduce.4 = bf16[6144,64]{0,1:T(8,128)(2,1)S(1)} all-reduce(f32[6144,64]{0,1:T(8,128)S(1)} %fusion.9), channel_id=1, replica_groups=mesh['dp'=8,'mp'=4] {'dp','mp'}, use_global_device_ids=true, to_apply=%region_4.5 | all-reduce | flops 393216 | bytes 2359296 | tf_op jit(solution)/shard_map/psum | solution.py:42
  232.8 0.0 copy-start.2
  232.8 0.0 copy-start.3
  232.8 7.8 %fusion.1 = bf16[1,768,6144]{2,1,0:T(8,128)(2,1)} fusion(bf16[768,64]{0,1:T(8,128)(2,1)S(1)} %convolution_convert_fusion, bf16[6144,64]{0,1:T(8,128)(2,1)S(1)} %all-reduce.4, bf16[768,6144]{1,0:T(8,128)(2,1)} %copy-done.1), kind=kOutput, calls=%fused_computation.3 | convolution fusion | flops 622854144 | bytes 19759104 | tf_op jit(solution)/shard_map/dot_general | solution.py:48
  240.7 0.0 copy-done.2
  240.7 0.0 copy-done.3
  240.7 1.9 multiply_add_fusion
  (2 shorter events, 0.0 us)
Async XLA Ops:
  7.2 51.5 %copy-start = (bf16[512,768]{1,0:T(8,128)(2,1)S(1)}, bf16[512,768]{1,0:T(8,128)(2,1)}, u32[]{:S(2)}) copy-start(bf16[512,768]{1,0:T(8,128)(2,1)} %param.5) | copy-start | bytes 2359300
  7.2 51.5 %all-gather.2.cloned.1.call-start = ((), (), s32[]{:S(2)}) async-start(), calls=%async_computation | async-start | bytes 7864320 | tf_op jit(solution)/shard_map/all_gather | solution.py:20
  7.9 64.2 %copy-start.4 = (bf16[6144,64]{0,1:T(8,128)(2,1)S(1)}, bf16[6144,64]{0,1:T(8,128)(2,1)}, u32[]{:S(2)}) copy-start(bf16[6144,64]{0,1:T(8,128)(2,1)} %param.8) | copy-start | bytes 2359300
  7.9 138.7 %all-reduce.3.cloned.1.call-start = ((), (), s32[]{:S(2)}) async-start(), calls=%async_computation.1 | async-start | bytes 393216 | tf_op jit(solution)/shard_map/psum | solution.py:26
  68.3 3.7 %copy-start.1 = (bf16[768,6144]{1,0:T(8,128)(2,1)}, bf16[768,6144]{1,0:T(8,128)(2,1)S(1)}, u32[]{:S(2)}) copy-start(bf16[768,6144]{1,0:T(8,128)(2,1)S(1)} %fusion) | copy-start | bytes 28311556
  232.8 7.8 %copy-start.2 = (bf16[6144,64]{0,1:T(8,128)(2,1)}, bf16[6144,64]{0,1:T(8,128)(2,1)S(1)}, u32[]{:S(2)}) copy-start(bf16[6144,64]{0,1:T(8,128)(2,1)S(1)} %all-reduce.4) | copy-start | bytes 2359300
  232.8 7.8 %copy-start.3 = (f32[768,768]{1,0:T(8,128)S(1)}, f32[768,768]{1,0:T(8,128)}, u32[]{:S(2)}) copy-start(f32[768,768]{1,0:T(8,128)} %param.9) | copy-start | bytes 7077892
Sparse Core Ops, SparseCore 0:
  9.5 49.0 all-gather.1
  75.9 70.6 all-reduce.2
where the time goes:
time: 250 us; the launch traced here: 249 us
  waiting for transfers between devices  122 us (49%)
  blocking collectives  66 us (26%)
  matrix products  31.1 us (12%)
  between operations  14.2 us (6%)
  other arithmetic  12.1 us (5%)
  local copies, waits for them, and re-layouts  3.84 us (2%)
    psum x1, waiting for transfers between devices, local(): left_sketch = lax.psum(local_left, 'dp')  70.8 us
    psum x1, blocking collectives, local(): right_sketch = lax.psum(local_right, ('dp', 'mp'))  55.7 us
    all_gather x1, waiting for transfers between devices, local(): lax.all_gather(out_grads, 'mp', axis=1, tiled=True)  50.7 us
    psum x1, blocking collectives, local(): gram_matrix = lax.psum(gram_local, 'mp')  10.3 us
    dot_general x1, matrix products, local(): lax.dot_general(activations, lax.all_gather(out_grads, 'mp', axis=1, tile...  9.64 us
    dot_general x1, matrix products, local(): lax.dot_general(basis_rows, next_sketch, (((1,), (1,)), ((), ())), prefer...  7.81 us
    another operation x3, other arithmetic, local(): factor = jnp.linalg.cholesky(gram_matrix)  6.52 us
    another operation x2, other arithmetic, local(): jax.scipy.linalg.solve_triangular(factor, left_sketch.T, lower=True)  5.55 us
  transfers between devices with their start and end apart: 2, of which 2 were waited for; matrix products, arithmetic and copies ran while one was open for 0% of the time, Pallas kernels for 0%

commit v1 on v0

--- a/solution.py
+++ b/solution.py
@@ -4,6 +4,15 @@
 from jax.sharding import PartitionSpec as P
 
 beta_decay = 0.9
+
+
+def order_cubes(block_in):
+    mesh_name = "dp"
+    dev_n = lax.axis_size(mesh_name)
+    row_out = block_in
+    for s in [[(j0, j0 ^ c) for j0 in range(dev_n)] for c in (1, 2, 4, 8, 16) if c < dev_n]:
+        row_out = row_out + lax.ppermute(row_out, axis_name=mesh_name, perm=s)
+    return row_out
 
 
 def update_momentum(momentum, basis_rows, sketch_block):
@@ -23,7 +32,7 @@
     )
     accumulated = (product + own_error.astype(jnp.float32)).astype(jnp.bfloat16)
     local_left = jnp.dot(accumulated, sketch, preferred_element_type=jnp.float32)
-    left_sketch = lax.psum(local_left, "dp")
+    left_sketch = order_cubes(local_left)
     gram_local = jnp.dot(
         left_sketch.T,
         left_sketch,

time: 250 us -> 201 us (0.80)
  waiting for transfers between devices: 122 us -> 69.8 us
  starting transfers between devices: 0.08 us -> 5.59 us
  matrix products: 31.1 us -> 28.4 us
    psum x1 -> x0, waiting for transfers between devices: 70.8 us -> none  [local(): left_sketch = lax.psum(local_left, 'dp')]
    ppermute x0 -> x3, waiting for transfers between devices: none -> 18.3 us  [order_cubes(): row_out = row_out + lax.ppermute(row_out, axis_name=mesh_name, perm=s)]
    ppermute x0 -> x3, starting transfers between devices: none -> 5.55 us  [order_cubes(): row_out = row_out + lax.ppermute(row_out, axis_name=mesh_name, perm=s)]
  transfers between devices with their start and end apart: 2 -> 4, of which waited for: 2 -> 4; matrix products, arithmetic and copies ran while one was open for 0% -> 0% of each run, Pallas kernels for 0% -> 0%
where the time goes in v1:
time: 201 us; the launch traced here: 200 us
  waiting for transfers between devices  69.8 us (35%)
  blocking collectives  66.4 us (33%)
  matrix products  28.4 us (14%)
  between operations  14.2 us (7%)
  other arithmetic  12.2 us (6%)
  starting transfers between devices  5.59 us (3%)
  local copies, waits for them, and re-layouts  3.84 us (2%)
    psum x1, blocking collectives, local(): right_sketch = lax.psum(local_right, ('dp', 'mp'))  56.2 us
    all_gather x1, waiting for transfers between devices, local(): lax.all_gather(out_grads, 'mp', axis=1, tiled=True)  50.7 us
    ppermute x3, waiting for transfers between devices, order_cubes(): row_out = row_out + lax.ppermute(row_out, axis_name=mesh_name, perm=s)  18.3 us
    psum x1, blocking collectives, local(): gram_matrix = lax.psum(gram_local, 'mp')  10.3 us
    dot_general x1, matrix products, local(): lax.dot_general(activations, lax.all_gather(out_grads, 'mp', axis=1, tile...  9.64 us
    dot_general x1, matrix products, local(): lax.dot_general(basis_rows, next_sketch, (((1,), (1,)), ((), ())), prefer...  7.81 us
    another operation x3, other arithmetic, local(): factor = jnp.linalg.cholesky(gram_matrix)  6.52 us
    ppermute x3, starting transfers between devices, order_cubes(): row_out = row_out + lax.ppermute(row_out, axis_name=mesh_name, perm=s)  5.55 us
  transfers between devices with their start and end apart: 4, of which 4 were waited for; matrix products, arithmetic and copies ran while one was open for 0% of the time, Pallas kernels for 0%

profile of v1, /device:TPU:0, one launch (start us, length us, event | category | flops | bytes accessed | tf_op | source)
XLA Modules:
  0.0 200.4 jit_solution(16785870263749307749)
XLA Ops:
  7.2 0.0 copy-start
  7.2 0.0 all-gather.2.cloned.1.call-start
  7.2 0.7 all-gather.2.cloned.1.call-update
  7.9 0.0 copy-start.4
  7.9 50.7 %all-gather.2.cloned.1.call-done = bf16[512,6144]{1,0:T(8,128)(2,1)} async-done(((bf16[512,1536]{1,0:T(8,128)(2,1)}), bf16[512,6144]{1,0:T(8,128)(2,1)}) %all-gather.2.cloned.1.call-update) | async-done | bytes 6291472 | tf_op jit(solution)/shard_map/all_gather | solution.py:29
  58.7 0.0 copy-done
  58.7 9.6 %fusion = bf16[768,6144]{1,0:T(8,128)(2,1)S(1)} fusion(bf16[1,768,6144]{2,1,0:T(8,128)(2,1)} %param.7, bf16[512,768]{1,0:T(8,128)(2,1)S(1)} %copy-done, bf16[512,6144]{1,0:T(8,128)(2,1)} %all-gather.2.cloned.1.call-done), kind=kOutput, calls=%fused_computation.1 | convolution fusion | flops 4845993984 | bytes 25952256 | tf_op jit(solution)/shard_map/dot_general | solution.py:27
  68.3 0.0 copy-start.1
  68.3 3.7 %copy-done.1 = bf16[768,6144]{1,0:T(8,128)(2,1)} copy-done((bf16[768,6144]{1,0:T(8,128)(2,1)}, bf16[768,6144]{1,0:T(8,128)(2,1)S(1)}, u32[]{:S(2)}) %copy-start.1) | copy-done | bytes 9437208
  72.1 0.0 copy-done.4
  72.1 3.0 %fusion.7 = f32[768,64]{0,1:T(8,128)S(1)} fusion(bf16[768,6144]{1,0:T(8,128)(2,1)S(1)} %fusion, bf16[6144,64]{0,1:T(8,128)(2,1)S(1)} %copy-done.4), kind=kOutput, calls=%fused_computation.17 | convolution fusion | flops 603979776 | bytes 10420224 | tf_op jit(solution)/shard_map/dot_general | solution.py:34
  75.0 1.5 collective-permute-start
  76.6 5.6 %collective-permute-done = f32[768,64]{0,1:T(8,128)S(1)} collective-permute-done((f32[768,64]{0,1:T(8,128)S(1)}, f32[768,64]{0,1:T(8,128)S(1)}, u32[]{:S(2)}, u32[]{:S(2)}) %collective-permute-start) | collective-permute-done | bytes 196640 | tf_op jit(solution)/shard_map/ppermute | solution.py:14
  82.2 1.6 collective-permute-start.1
  83.7 4.7 %collective-permute-done.1 = f32[768,64]{0,1:T(8,128)S(1)} collective-permute-done((f32[768,64]{0,1:T(8,128)S(1)}, f32[768,64]{0,1:T(8,128)S(1)}, u32[]{:S(2)}, u32[]{:S(2)}) %collective-permute-start.1) | collective-permute-done | bytes 196640 | tf_op jit(solution)/shard_map/ppermute | solution.py:14
  88.5 2.5 %collective-permute-start.2 = (f32[768,64]{0,1:T(8,128)S(1)}, f32[768,64]{0,1:T(8,128)S(1)}, u32[]{:S(2)}, u32[]{:S(2)}) collective-permute-start(f32[768,64]{0,1:T(8,128)S(1)} %add.36), channel_id=1, source_target_pairs={{0,16},{4,20},{8,24},{12,28},{16,0},{20,4},{24,8},{28,12},{1,17},{... | collective-permute-start | bytes 589832 | tf_op jit(solution)/shard_map/ppermute | solution.py:14
  90.9 8.1 %collective-permute-done.2 = f32[768,64]{0,1:T(8,128)S(1)} collective-permute-done((f32[768,64]{0,1:T(8,128)S(1)}, f32[768,64]{0,1:T(8,128)S(1)}, u32[]{:S(2)}, u32[]{:S(2)}) %collective-permute-start.2) | collective-permute-done | bytes 196640 | tf_op jit(solution)/shard_map/ppermute | solution.py:14
  99.0 0.3 fusion.8
  99.3 10.3 %psum.14 = f32[64,64]{0,1:T(8,128)S(1)} all-reduce(f32[64,64]{0,1:T(8,128)S(1)} %fusion.8), channel_id=1, replica_groups=mesh['dp'=8,'mp'=4] {'mp'}, use_global_device_ids=true, to_apply=%region_0.0 | all-reduce | flops 4096 | bytes 32768 | tf_op jit(solution)/shard_map/psum | solution.py:42
  109.6 0.1 copy.9
  109.7 5.8 %cholesky.16 = f32[64,64]{1,0:T(8,128)S(1)} custom-call(f32[64,64]{1,0:T(8,128)S(1)} %fusion.5), custom_call_target="Cholesky" | custom-call | tf_op jit(solution)/shard_map/jit(cholesky)/cholesky | solution.py:43
  115.6 0.6 compare_reduce_fusion
  116.2 0.7 fusion.3
  116.9 4.9 %custom-call.7 = f32[1,64,64]{1,2,0:T(8,128)S(1)} custom-call(f32[1,64,64]{2,1,0:T(8,128)S(1)} %fusion.3), custom_call_target="InvertDiagBlocksLowerTriangular" | custom-call | tf_op jit(solution)/shard_map/jit(_solve_triangular)/triangular_solve | solution.py:44
  121.8 0.4 convolution_convert_fusion
  122.2 5.4 %fusion.9 = f32[6144,64]{0,1:T(8,128)S(1)} fusion(bf16[768,64]{0,1:T(8,128)(2,1)S(1)} %convolution_convert_fusion, bf16[768,6144]{1,0:T(8,128)(2,1)} %copy-done.1), kind=kOutput, calls=%fused_computation.19 | convolution fusion | flops 603979776 | bytes 11108352 | tf_op jit(solution)/shard_map/dot_general | solution.py:48
  127.6 56.2 %all-reduce.1 = bf16[6144,64]{0,1:T(8,128)(2,1)S(1)} all-reduce(f32[6144,64]{0,1:T(8,128)S(1)} %fusion.9), channel_id=1, replica_groups=mesh['dp'=8,'mp'=4] {'dp','mp'}, use_global_device_ids=true, to_apply=%region_3.4 | all-reduce | flops 393216 | bytes 2359296 | tf_op jit(solution)/shard_map/psum | solution.py:51
  183.8 0.0 copy-start.2
  183.8 0.0 copy-start.3
  183.8 7.8 %fusion.1 = bf16[1,768,6144]{2,1,0:T(8,128)(2,1)} fusion(bf16[768,64]{0,1:T(8,128)(2,1)S(1)} %convolution_convert_fusion, bf16[6144,64]{0,1:T(8,128)(2,1)S(1)} %all-reduce.1, bf16[768,6144]{1,0:T(8,128)(2,1)} %copy-done.1), kind=kOutput, calls=%fused_computation.3 | convolution fusion | flops 622854144 | bytes 19759104 | tf_op jit(solution)/shard_map/dot_general | solution.py:57
  191.6 0.0 copy-done.2
  191.6 0.0 copy-done.3
  191.6 1.9 multiply_add_fusion
  (5 shorter events, 0.1 us)
Async XLA Ops:
  7.2 51.5 %copy-start = (bf16[512,768]{1,0:T(8,128)(2,1)S(1)}, bf16[512,768]{1,0:T(8,128)(2,1)}, u32[]{:S(2)}) copy-start(bf16[512,768]{1,0:T(8,128)(2,1)} %param.5) | copy-start | bytes 2359300
  7.2 51.5 %all-gather.2.cloned.1.call-start = ((), (), s32[]{:S(2)}) async-start(), calls=%async_computation | async-start | bytes 7864320 | tf_op jit(solution)/shard_map/all_gather | solution.py:29
  7.9 64.2 %copy-start.4 = (bf16[6144,64]{0,1:T(8,128)(2,1)S(1)}, bf16[6144,64]{0,1:T(8,128)(2,1)}, u32[]{:S(2)}) copy-start(bf16[6144,64]{0,1:T(8,128)(2,1)} %param.8) | copy-start | bytes 2359300
  68.3 3.7 %copy-start.1 = (bf16[768,6144]{1,0:T(8,128)(2,1)}, bf16[768,6144]{1,0:T(8,128)(2,1)S(1)}, u32[]{:S(2)}) copy-start(bf16[768,6144]{1,0:T(8,128)(2,1)S(1)} %fusion) | copy-start | bytes 28311556
  75.0 7.1 %collective-permute-start = (f32[768,64]{0,1:T(8,128)S(1)}, f32[768,64]{0,1:T(8,128)S(1)}, u32[]{:S(2)}, u32[]{:S(2)}) collective-permute-start(f32[768,64]{0,1:T(8,128)S(1)} %fusion.7), channel_id=1, source_target_pairs={{0,4},{4,0},{8,12},{12,8},{16,20},{20,16},{24,28},{28,24},{1,5},{5... | collective-permute-start | bytes 589832 | tf_op jit(solution)/shard_map/ppermute | solution.py:14
  82.2 6.3 %collective-permute-start.1 = (f32[768,64]{0,1:T(8,128)S(1)}, f32[768,64]{0,1:T(8,128)S(1)}, u32[]{:S(2)}, u32[]{:S(2)}) collective-permute-start(f32[768,64]{0,1:T(8,128)S(1)} %add.35), channel_id=1, source_target_pairs={{0,8},{4,12},{8,0},{12,4},{16,24},{20,28},{24,16},{28,20},{1,9},{5... | collective-permute-start | bytes 589832 | tf_op jit(solution)/shard_map/ppermute | solution.py:14
  88.5 10.5 %collective-permute-start.2 = (f32[768,64]{0,1:T(8,128)S(1)}, f32[768,64]{0,1:T(8,128)S(1)}, u32[]{:S(2)}, u32[]{:S(2)}) collective-permute-start(f32[768,64]{0,1:T(8,128)S(1)} %add.36), channel_id=1, source_target_pairs={{0,16},{4,20},{8,24},{12,28},{16,0},{20,4},{24,8},{28,12},{1,17},{... | collective-permute-start | bytes 589832 | tf_op jit(solution)/shard_map/ppermute | solution.py:14
  183.8 7.8 %copy-start.2 = (bf16[6144,64]{0,1:T(8,128)(2,1)}, bf16[6144,64]{0,1:T(8,128)(2,1)S(1)}, u32[]{:S(2)}) copy-start(bf16[6144,64]{0,1:T(8,128)(2,1)S(1)} %all-reduce.1) | copy-start | bytes 2359300
  183.8 7.8 %copy-start.3 = (f32[768,768]{1,0:T(8,128)S(1)}, f32[768,768]{1,0:T(8,128)}, u32[]{:S(2)}) copy-start(f32[768,768]{1,0:T(8,128)} %param.9) | copy-start | bytes 7077892
Sparse Core Ops, SparseCore 0:
  9.5 49.0 all-gather.1
